TPU v7x, 1024 devices: a whole 4x4x32 slice. The times are simulated.
1024 devices in a mesh: grp: 8 (over x, core), dev: 128 (over z, y).
Axes of the slice: x: 4, y: 4, z: 32, core: 2. Of those that a mesh axis runs over, the one named last changes fastest.
Arguments:
- node_latent: bfloat16 [1024, 128, 256], P(('grp', 'dev')), may hold values from -6 to 6
- edge_latent: bfloat16 [1024, 384, 256], P(('grp', 'dev')), may hold values from -6 to 6
- cut_latent: bfloat16 [1024, 5, 64, 256], P(('grp', 'dev')), may hold values from -6 to 6
- node_cotangent: bfloat16 [1024, 128, 256], P(('grp', 'dev')), may hold values from -6 to 6
- edge_sender: int32 [1024, 384], P(('grp', 'dev')), may hold values from 0 to 127, as said below
- edge_receiver: int32 [1024, 384], P(('grp', 'dev')), may hold values from 0 to 127, as said below
- boundary_rows: int32 [1024, 5, 16], P(('grp', 'dev')), may hold values from 0 to 127, as said below
- cut_slot: int32 [1024, 5, 64], P(('grp', 'dev')), may hold values from 0 to 15
- cut_receiver: int32 [1024, 5, 64], P(('grp', 'dev')), may hold values from 0 to 127, as said below
- node_count: int32 [1024], P(('grp', 'dev')), may hold values from 64 to 128, as said below
- edge_count: int32 [1024], P(('grp', 'dev')), may hold values from 192 to 384, as said below
- edge_first: bfloat16 [768, 256], replicated, may hold values from -0.21875 to 0.21875
- edge_second: bfloat16 [256, 256], replicated, may hold values from -0.375 to 0.375
- edge_gain: float32 [256], replicated, may hold values from 0.1 to 1.9
- node_first: bfloat16 [512, 256], replicated, may hold values from -0.25 to 0.25
- node_second: bfloat16 [256, 256], replicated, may hold values from -0.375 to 0.375
- node_gain: float32 [256], replicated, may hold values from 0.1 to 1.9
Outputs:
- updated_nodes: bfloat16 [1024, 128, 256], P(('grp', 'dev'))
- node_gradient: bfloat16 [1024, 128, 256], P(('grp', 'dev'))
- edge_gradient: bfloat16 [1024, 384, 256], P(('grp', 'dev'))
- cut_gradient: bfloat16 [1024, 5, 64, 256], P(('grp', 'dev'))
Inputs may be any that keep to these rules, and one draw needn't show every extreme that they name: Nodes at or beyond a partition's node_count are padding. Inner edges at or beyond a partition's edge_count are padding. `edge_sender`: a node of the partition below its node_count. `edge_receiver`: a node of the partition below its node_count. `boundary_rows`: a node of the partition below its node_count; a node may stand more than once. `cut_receiver`: a node of the partition below its node_count.
All inputs are finite; a program needn't handle non-finite values.
Results may differ from a plain program's by a relative error of at most 0.0095.
Values may be sent and summed in bfloat16 or wider, within the bound.
A program may use at most 32 MiB of HBM per device.

v0:
```python
import jax
import jax.numpy as jnp
from jax import lax
from jax.sharding import PartitionSpec as P

ROUNDS = 5


epsilon = 1e-05


def partner(shard, axis, apart):
    return lax.ppermute(shard, axis, [(i, i ^ 1 << apart) for i in range(lax.axis_size(axis))])


def layer_norm(values, gain):
    centre = jnp.mean(values, axis=-1, keepdims=True)
    centred = values - centre
    variance = jnp.mean(centred * centred, axis=-1, keepdims=True)
    inverse = 1.0 / jnp.sqrt(variance + epsilon)
    normed = centred * inverse
    return (normed * gain, normed, inverse)


def norm_backward(upstream, gain, normed, inverse):
    scaled = upstream * gain
    first_mean = jnp.mean(scaled, axis=-1, keepdims=True)
    second_mean = jnp.mean(scaled * normed, axis=-1, keepdims=True)
    return inverse * (scaled - first_mean - normed * second_mean)


def silu_slope(values):
    sigmoid = jax.nn.sigmoid(values)
    return sigmoid * (1.0 + values * (1.0 - sigmoid))


def slot_total(slot_ids, values, count):
    table = (slot_ids[None, :] == jnp.arange(count)[:, None]).astype(jnp.float32)
    return jnp.dot(
        table, values, precision=lax.Precision.HIGHEST, preferred_element_type=jnp.float32
    )


def swap_rows(outgoing, round_index):
    if round_index < 2:
        return partner(outgoing, "grp", round_index)
    return partner(outgoing, "dev", round_index - 2)


def swap_slopes(payload, round_index):
    if round_index < 2:
        return partner((payload[0], payload[1]), "grp", round_index)
    return partner((payload[0], payload[1]), "dev", round_index - 2)


def shards(
    node_latent,
    edge_latent,
    cut_latent,
    node_cotangent,
    edge_sender,
    edge_receiver,
    boundary_rows,
    cut_slot,
    cut_receiver,
    node_count,
    edge_count,
    edge_first,
    edge_second,
    edge_gain,
    node_first,
    node_second,
    node_gain,
):
    nodes = node_latent[0]
    edges = edge_latent[0]
    cut_edges = cut_latent[0]
    cotangent = node_cotangent[0]
    senders = edge_sender[0]
    receivers_local = edge_receiver[0]
    boundary = boundary_rows[0]
    slots = cut_slot[0]
    cut_targets = cut_receiver[0]
    width = nodes.shape[1]
    node_rows = nodes.shape[0]
    edge_rows = edges.shape[0]
    send_rows = boundary.shape[1]
    valid = (jnp.arange(node_rows) < node_count[0]).astype(jnp.float32)[:, None]
    used = (jnp.arange(edge_rows) < edge_count[0]).astype(jnp.float32)
    sender_block = edge_first[width : 2 * width]
    other_block = jnp.concatenate([edge_first[:width], edge_first[2 * width :]], 0)
    cut_flat = cut_targets.reshape(-1)
    pieces = []
    for round_index in range(ROUNDS):
        outgoing = nodes[boundary[round_index]]
        arrived = swap_rows(outgoing, round_index)
        pieces.append(
            jnp.concatenate(
                [
                    nodes[cut_targets[round_index]],
                    arrived[slots[round_index]],
                    cut_edges[round_index],
                ],
                1,
            )
        )
    local_input = jnp.concatenate([nodes[receivers_local], nodes[senders], edges], 1)
    pre_local = jnp.dot(local_input, edge_first, preferred_element_type=jnp.float32)
    pre_cut = jnp.dot(jnp.concatenate(pieces, 0), edge_first, preferred_element_type=jnp.float32)
    pre_edge = jnp.concatenate([pre_local, pre_cut], 0)
    receivers = jnp.concatenate([receivers_local, cut_flat])
    mask = jnp.concatenate([used, jnp.ones((cut_flat.shape[0],), jnp.float32)])[:, None]
    act_edge = jax.nn.silu(pre_edge).astype(jnp.bfloat16)
    out_edge = jnp.dot(act_edge, edge_second, preferred_element_type=jnp.float32)
    normed_edge, edge_normed, edge_inverse = layer_norm(out_edge, edge_gain)
    message = normed_edge * mask
    received_sum = jnp.zeros((node_rows, width), jnp.float32).at[receivers].add(message)
    node_input = jnp.concatenate([nodes, received_sum.astype(jnp.bfloat16)], 1)
    pre_node = jnp.dot(node_input, node_first, preferred_element_type=jnp.float32)
    act_node = jax.nn.silu(pre_node).astype(jnp.bfloat16)
    out_node = jnp.dot(act_node, node_second, preferred_element_type=jnp.float32)
    normed_node, node_normed, node_inverse = layer_norm(out_node, node_gain)
    updated = ((nodes.astype(jnp.float32) + normed_node) * valid).astype(jnp.bfloat16)
    masked_cotangent = cotangent.astype(jnp.float32) * valid
    grad_out_node = norm_backward(masked_cotangent, node_gain, node_normed, node_inverse).astype(
        jnp.bfloat16
    )
    grad_act_node = jnp.dot(grad_out_node, node_second.T, preferred_element_type=jnp.float32)
    grad_pre_node = (grad_act_node * silu_slope(pre_node)).astype(jnp.bfloat16)
    grad_node_input = jnp.dot(grad_pre_node, node_first.T, preferred_element_type=jnp.float32)
    grad_message = grad_node_input[:, width:][receivers] * mask
    grad_out_edge = norm_backward(grad_message, edge_gain, edge_normed, edge_inverse).astype(
        jnp.bfloat16
    )
    grad_act_edge = jnp.dot(grad_out_edge, edge_second.T, preferred_element_type=jnp.float32)
    grad_pre_edge = (grad_act_edge * silu_slope(pre_edge)).astype(jnp.bfloat16)
    local_grad = jnp.dot(
        grad_pre_edge[:edge_rows], edge_first.T, preferred_element_type=jnp.float32
    )
    gradient = masked_cotangent + grad_node_input[:, :width]
    gradient = gradient.at[receivers_local].add(local_grad[:, :width])
    gradient = gradient.at[senders].add(local_grad[:, width : 2 * width])
    edge_gradient = local_grad[:, 2 * width :].astype(jnp.bfloat16)
    cut_pre = grad_pre_edge[edge_rows:]
    cut_grad = jnp.dot(cut_pre, other_block.T, preferred_element_type=jnp.float32)
    gradient = gradient.at[cut_flat].add(cut_grad[:, :width])
    cut_gradient = cut_grad[:, width:]
    per_round = cut_pre.reshape(ROUNDS, -1, width)
    for round_index in range(ROUNDS):
        arrived_grad, arrived_slots = swap_slopes(
            (per_round[round_index], slots[round_index]), round_index
        )
        sender_grad = jnp.dot(arrived_grad, sender_block.T, preferred_element_type=jnp.float32)
        gradient = gradient.at[boundary[round_index]].add(
            slot_total(arrived_slots, sender_grad, send_rows)
        )
    cut_gradient = cut_gradient.reshape(ROUNDS, -1, width).astype(jnp.bfloat16)
    return (
        updated[None],
        gradient.astype(jnp.bfloat16)[None],
        edge_gradient[None],
        cut_gradient[None],
    )


def solution(mesh):
    placed = (
        P(("grp", "dev"), None, None),
        P(("grp", "dev"), None, None),
        P(("grp", "dev"), None, None, None),
        P(("grp", "dev"), None, None),
        P(("grp", "dev"), None),
        P(("grp", "dev"), None),
        P(("grp", "dev"), None, None),
        P(("grp", "dev"), None, None),
        P(("grp", "dev"), None, None),
        P(("grp", "dev")),
        P(("grp", "dev")),
        P(),
        P(),
        P(),
        P(),
        P(),
        P(),
    )
    return jax.shard_map(
        shards,
        mesh=mesh,
        in_specs=placed,
        out_specs=(
            P(("grp", "dev"), None, None),
            P(("grp", "dev"), None, None),
            P(("grp", "dev"), None, None),
            P(("grp", "dev"), None, None, None),
        ),
        check_vma=False,
    )
```

profile of v0, /device:TPU:8, one launch (start us, length us, event | category | flops | bytes accessed | tf_op | source)
XLA Modules:
  0.0 124.5 jit_solution(6173814247657136573)
XLA Ops:
  2.9 1.9 %collective-permute-start = (bf16[16,256]{1,0:T(8,128)(2,1)S(1)}, bf16[16,256]{1,0:T(8,128)(2,1)S(1)}, u32[]{:S(2)}, u32[]{:S(2)}) collective-permute-start(bf16[16,256]{1,0:T(8,128)(2,1)S(1)} %gather_fusion.3), channel_id=1, source_target_pairs={{0,128},{128,0},{256,384},{384,256},{512,640},{640,512},{768,896},... | collective-permute-start | bytes 24584 | tf_op jit(solution)/shard_map/ppermute | solution.py:13
  6.3 3.4 %collective-permute-start.1 = (bf16[16,256]{1,0:T(8,128)(2,1)S(1)}, bf16[16,256]{1,0:T(8,128)(2,1)S(1)}, u32[]{:S(2)}, u32[]{:S(2)}) collective-permute-start(bf16[16,256]{1,0:T(8,128)(2,1)S(1)} %gather_fusion.6), channel_id=1, source_target_pairs={{0,256},{128,384},{256,0},{384,128},{512,768},{640,896},{768,512},... | collective-permute-start | bytes 24584 | tf_op jit(solution)/shard_map/ppermute | solution.py:13
  11.1 13.5 %collective-permute-start.2 = (bf16[16,256]{1,0:T(8,128)(2,1)S(1)}, bf16[16,256]{1,0:T(8,128)(2,1)S(1)}, u32[]{:S(2)}, u32[]{:S(2)}) collective-permute-start(bf16[16,256]{1,0:T(8,128)(2,1)S(1)} %gather_fusion.9), channel_id=1, source_target_pairs={{0,1},{1,0},{2,3},{3,2},{4,5},{5,4},{6,7},{7,6},{8,9},{9,8},{10,11... | collective-permute-start | bytes 24584 | tf_op jit(solution)/shard_map/ppermute | solution.py:13
  26.1 1.9 %collective-permute-start.3 = (bf16[16,256]{1,0:T(8,128)(2,1)S(1)}, bf16[16,256]{1,0:T(8,128)(2,1)S(1)}, u32[]{:S(2)}, u32[]{:S(2)}) collective-permute-start(bf16[16,256]{1,0:T(8,128)(2,1)S(1)} %gather_fusion.12), channel_id=1, source_target_pairs={{0,2},{1,3},{2,0},{3,1},{4,6},{5,7},{6,4},{7,5},{8,10},{9,11},{10,... | collective-permute-start | bytes 24584 | tf_op jit(solution)/shard_map/ppermute | solution.py:13
  29.4 1.9 %collective-permute-start.4 = (bf16[16,256]{1,0:T(8,128)(2,1)S(1)}, bf16[16,256]{1,0:T(8,128)(2,1)S(1)}, u32[]{:S(2)}, u32[]{:S(2)}) collective-permute-start(bf16[16,256]{1,0:T(8,128)(2,1)S(1)} %gather_fusion.15), channel_id=1, source_target_pairs={{0,4},{1,5},{2,6},{3,7},{4,0},{5,1},{6,2},{7,3},{8,12},{9,13},{10,... | collective-permute-start | bytes 24584 | tf_op jit(solution)/shard_map/ppermute | solution.py:13
  37.9 2.1 %gather_fusion.1 = bf16[384,256]{1,0:T(8,128)(2,1)S(1)} fusion(bf16[128,256]{1,0:T(8,128)(2,1)S(1)} %bitcast.133, s32[1024]{0:T(1024)S(1)} %get-tuple-element.48), kind=kCustom, calls=%fused_computation.1 | custom fusion | bytes 394752 | tf_op jit(solution)/shard_map/gather | solution.py:107
  40.0 2.1 %gather_fusion = bf16[384,256]{1,0:T(8,128)(2,1)S(1)} fusion(bf16[128,256]{1,0:T(8,128)(2,1)S(1)} %bitcast.134, s32[1024]{0:T(1024)S(1)} %pad_clamp_fusion.17), kind=kCustom, calls=%fused_computation | custom fusion | bytes 394752 | tf_op jit(solution)/shard_map/gather | solution.py:107
  46.8 2.1 %collective-permute-start.5 = (s32[64]{0:T(128)S(1)}, s32[64]{0:T(128)S(1)}, u32[]{:S(2)}, u32[]{:S(2)}) collective-permute-start(s32[64]{0:T(128)S(1)} %get-tuple-element.24), channel_id=1, source_target_pairs={{0,128},{128,0},{256,384},{384,256},{512,640},{640,512},{768,896},... | collective-permute-start | bytes 776 | tf_op jit(solution)/shard_map/ppermute | solution.py:13
  49.6 3.7 %collective-permute-start.7 = (s32[64]{0:T(128)S(1)}, s32[64]{0:T(128)S(1)}, u32[]{:S(2)}, u32[]{:S(2)}) collective-permute-start(s32[64]{0:T(128)S(1)} %get-tuple-element.25), channel_id=1, source_target_pairs={{0,256},{128,384},{256,0},{384,128},{512,768},{640,896},{768,512},... | collective-permute-start | bytes 776 | tf_op jit(solution)/shard_map/ppermute | solution.py:13
  54.1 2.1 %collective-permute-start.9 = (s32[64]{0:T(128)S(1)}, s32[64]{0:T(128)S(1)}, u32[]{:S(2)}, u32[]{:S(2)}) collective-permute-start(s32[64]{0:T(128)S(1)} %get-tuple-element.26), channel_id=1, source_target_pairs={{0,1},{1,0},{2,3},{3,2},{4,5},{5,4},{6,7},{7,6},{8,9},{9,8},{10,11... | collective-permute-start | bytes 776 | tf_op jit(solution)/shard_map/ppermute | solution.py:13
  57.0 5.4 %collective-permute-start.11 = (s32[64]{0:T(128)S(1)}, s32[64]{0:T(128)S(1)}, u32[]{:S(2)}, u32[]{:S(2)}) collective-permute-start(s32[64]{0:T(128)S(1)} %get-tuple-element.27), channel_id=1, source_target_pairs={{0,2},{1,3},{2,0},{3,1},{4,6},{5,7},{6,4},{7,5},{8,10},{9,11},{10,... | collective-permute-start | bytes 776 | tf_op jit(solution)/shard_map/ppermute | solution.py:13
  64.9 6.7 %scatter_custom_fusion = f32[128,256]{1,0:T(8,128)S(1)} fusion(s32[704]{0:T(1024)S(1)} %fusion.95, f32[704,256]{1,0:T(8,128)S(1)} %get-tuple-element.44, f32[704]{0:T(1024)S(1)} %pad_convert_fusion, f32[256]{0:T(256)S(1)} %copy-done.4, f32[704]{0:T(1024)S(1)} %add_rsqrt_fusion, f32[704]{0:T(1024)S(1)} %broadcast_multiply_fusion.2, f32[]{:T(128)} %constant.11.clone.1), kind=kCustom, calls=%fused_computation.36 | custom fusion | flops 901120 | bytes 865284 | tf_op jit(solution)/shard_map/scatter-add | solution.py:117
  73.6 2.2 %gather_fusion.17 = f32[704,256]{1,0:T(8,128)S(1)} fusion(f32[128,256]{1,0:T(8,128)S(1)} %get-tuple-element.15, s32[1024]{0:T(1024)S(1)} %get-tuple-element.47), kind=kCustom, calls=%fused_computation.17 | custom fusion | bytes 1444608 | tf_op jit(solution)/shard_map/gather | solution.py:131
  78.2 1.9 %collective-permute-start.6 = (bf16[64,256]{1,0:T(8,128)(2,1)S(1)}, bf16[64,256]{1,0:T(8,128)(2,1)S(1)}, u32[]{:S(2)}, u32[]{:S(2)}) collective-permute-start(bf16[64,256]{1,0:T(8,128)(2,1)S(1)} %get-tuple-element.14), channel_id=1, source_target_pairs={{0,128},{128,0},{256,384},{384,256},{512,640},{640,512},{768,896},... | collective-permute-start | bytes 98312 | tf_op jit(solution)/shard_map/ppermute | solution.py:13
  81.1 2.9 %scatter_custom_fusion.1 = f32[128,256]{1,0:T(8,128)S(1)} fusion(f32[128,256]{1,0:T(8,128)S(1)} %get-tuple-element.16, s32[384]{0:T(512)S(1)} %fusion.96, f32[384,768]{1,0:T(8,128)S(1)} %fusion.35), kind=kCustom, calls=%fused_computation.53 | custom fusion | flops 98304 | bytes 524288 | tf_op jit(solution)/shard_map/scatter-add | solution.py:141
  84.0 2.7 %scatter_custom_fusion.2 = f32[128,256]{1,0:T(8,128)S(1)} fusion(f32[128,256]{1,0:T(8,128)S(1)} %scatter_custom_fusion.1, s32[384]{0:T(512)S(1)} %fusion.97, f32[384,768]{1,0:T(8,128)S(1)} %fusion.35), kind=kCustom, calls=%fused_computation.51 | custom fusion | flops 98304 | bytes 524288 | tf_op jit(solution)/shard_map/scatter-add | solution.py:142
  87.5 2.4 %scatter_custom_fusion.3 = f32[128,256]{1,0:T(8,128)S(1)} fusion(f32[128,256]{1,0:T(8,128)S(1)} %scatter_custom_fusion.2, s32[320]{0:T(512)S(1)} %fusion.98, f32[320,512]{1,0:T(8,128)S(1)} %fusion.30), kind=kCustom, calls=%fused_computation.67 | custom fusion | flops 81920 | bytes 458752 | tf_op jit(solution)/shard_map/scatter-add | solution.py:146
  89.9 2.1 %collective-permute-start.8 = (bf16[64,256]{1,0:T(8,128)(2,1)S(1)}, bf16[64,256]{1,0:T(8,128)(2,1)S(1)}, u32[]{:S(2)}, u32[]{:S(2)}) collective-permute-start(bf16[64,256]{1,0:T(8,128)(2,1)S(1)} %get-tuple-element.13), channel_id=1, source_target_pairs={{0,256},{128,384},{256,0},{384,128},{512,768},{640,896},{768,512},... | collective-permute-start | bytes 98312 | tf_op jit(solution)/shard_map/ppermute | solution.py:13
  92.2 3.5 %collective-permute-done.8 = bf16[64,256]{1,0:T(8,128)(2,1)S(1)} collective-permute-done((bf16[64,256]{1,0:T(8,128)(2,1)S(1)}, bf16[64,256]{1,0:T(8,128)(2,1)S(1)}, u32[]{:S(2)}, u32[]{:S(2)}) %collective-permute-start.8) | collective-permute-done | bytes 32800 | tf_op jit(solution)/shard_map/ppermute | solution.py:13
  95.7 4.5 %collective-permute-start.10 = (bf16[64,256]{1,0:T(8,128)(2,1)S(1)}, bf16[64,256]{1,0:T(8,128)(2,1)S(1)}, u32[]{:S(2)}, u32[]{:S(2)}) collective-permute-start(bf16[64,256]{1,0:T(8,128)(2,1)S(1)} %get-tuple-element.12), channel_id=1, source_target_pairs={{0,1},{1,0},{2,3},{3,2},{4,5},{5,4},{6,7},{7,6},{8,9},{9,8},{10,11... | collective-permute-start | bytes 98312 | tf_op jit(solution)/shard_map/ppermute | solution.py:13
  102.1 1.9 %collective-permute-start.12 = (bf16[64,256]{1,0:T(8,128)(2,1)S(1)}, bf16[64,256]{1,0:T(8,128)(2,1)S(1)}, u32[]{:S(2)}, u32[]{:S(2)}) collective-permute-start(bf16[64,256]{1,0:T(8,128)(2,1)S(1)} %get-tuple-element.11), channel_id=1, source_target_pairs={{0,2},{1,3},{2,0},{3,1},{4,6},{5,7},{6,4},{7,5},{8,10},{9,11},{10,... | collective-permute-start | bytes 98312 | tf_op jit(solution)/shard_map/ppermute | solution.py:13
  104.2 5.2 %collective-permute-done.12 = bf16[64,256]{1,0:T(8,128)(2,1)S(1)} collective-permute-done((bf16[64,256]{1,0:T(8,128)(2,1)S(1)}, bf16[64,256]{1,0:T(8,128)(2,1)S(1)}, u32[]{:S(2)}, u32[]{:S(2)}) %collective-permute-start.12) | collective-permute-done | bytes 32800 | tf_op jit(solution)/shard_map/ppermute | solution.py:13
  109.4 3.9 %collective-permute-start.14 = (bf16[64,256]{1,0:T(8,128)(2,1)S(1)}, bf16[64,256]{1,0:T(8,128)(2,1)S(1)}, u32[]{:S(2)}, u32[]{:S(2)}) collective-permute-start(bf16[64,256]{1,0:T(8,128)(2,1)S(1)} %get-tuple-element.10), channel_id=1, source_target_pairs={{0,4},{1,5},{2,6},{3,7},{4,0},{5,1},{6,2},{7,3},{8,12},{9,13},{10,... | collective-permute-start | bytes 98312 | tf_op jit(solution)/shard_map/ppermute | solution.py:13
  115.2 3.9 %collective-permute-start.13 = (s32[64]{0:T(128)S(1)}, s32[64]{0:T(128)S(1)}, u32[]{:S(2)}, u32[]{:S(2)}) collective-permute-start(s32[64]{0:T(128)S(1)} %get-tuple-element.23), channel_id=1, source_target_pairs={{0,4},{1,5},{2,6},{3,7},{4,0},{5,1},{6,2},{7,3},{8,12},{9,13},{10,... | collective-permute-start | bytes 776 | tf_op jit(solution)/shard_map/ppermute | solution.py:13
  (124 shorter events, 37.7 us)
Async XLA Ops:
  0.6 71.0 %copy-start = (bf16[512,256]{1,0:T(8,128)(2,1)S(1)}, bf16[512,256]{1,0:T(8,128)(2,1)}, u32[]{:S(2)}) copy-start(bf16[512,256]{1,0:T(8,128)(2,1)} %param.31) | copy-start | bytes 786436
  0.6 37.3 %copy-start.1 = (bf16[1,128,256]{2,1,0:T(8,128)(2,1)S(1)}, bf16[1,128,256]{2,1,0:T(8,128)(2,1)}, u32[]{:S(2)}) copy-start(bf16[1,128,256]{2,1,0:T(8,128)(2,1)} %param.17) | copy-start | bytes 196612
  2.9 43.9 %collective-permute-start = (bf16[16,256]{1,0:T(8,128)(2,1)S(1)}, bf16[16,256]{1,0:T(8,128)(2,1)S(1)}, u32[]{:S(2)}, u32[]{:S(2)}) collective-permute-start(bf16[16,256]{1,0:T(8,128)(2,1)S(1)} %gather_fusion.3), channel_id=1, source_target_pairs={{0,128},{128,0},{256,384},{384,256},{512,640},{640,512},{768,896},... | collective-permute-start | bytes 24584 | tf_op jit(solution)/shard_map/ppermute | solution.py:13
  6.3 43.4 %collective-permute-start.1 = (bf16[16,256]{1,0:T(8,128)(2,1)S(1)}, bf16[16,256]{1,0:T(8,128)(2,1)S(1)}, u32[]{:S(2)}, u32[]{:S(2)}) collective-permute-start(bf16[16,256]{1,0:T(8,128)(2,1)S(1)} %gather_fusion.6), channel_id=1, source_target_pairs={{0,256},{128,384},{256,0},{384,128},{512,768},{640,896},{768,512},... | collective-permute-start | bytes 24584 | tf_op jit(solution)/shard_map/ppermute | solution.py:13
  11.1 43.0 %collective-permute-start.2 = (bf16[16,256]{1,0:T(8,128)(2,1)S(1)}, bf16[16,256]{1,0:T(8,128)(2,1)S(1)}, u32[]{:S(2)}, u32[]{:S(2)}) collective-permute-start(bf16[16,256]{1,0:T(8,128)(2,1)S(1)} %gather_fusion.9), channel_id=1, source_target_pairs={{0,1},{1,0},{2,3},{3,2},{4,5},{5,4},{6,7},{7,6},{8,9},{9,8},{10,11... | collective-permute-start | bytes 24584 | tf_op jit(solution)/shard_map/ppermute | solution.py:13
  26.1 30.9 %collective-permute-start.3 = (bf16[16,256]{1,0:T(8,128)(2,1)S(1)}, bf16[16,256]{1,0:T(8,128)(2,1)S(1)}, u32[]{:S(2)}, u32[]{:S(2)}) collective-permute-start(bf16[16,256]{1,0:T(8,128)(2,1)S(1)} %gather_fusion.12), channel_id=1, source_target_pairs={{0,2},{1,3},{2,0},{3,1},{4,6},{5,7},{6,4},{7,5},{8,10},{9,11},{10,... | collective-permute-start | bytes 24584 | tf_op jit(solution)/shard_map/ppermute | solution.py:13
  29.4 33.6 %collective-permute-start.4 = (bf16[16,256]{1,0:T(8,128)(2,1)S(1)}, bf16[16,256]{1,0:T(8,128)(2,1)S(1)}, u32[]{:S(2)}, u32[]{:S(2)}) collective-permute-start(bf16[16,256]{1,0:T(8,128)(2,1)S(1)} %gather_fusion.15), channel_id=1, source_target_pairs={{0,4},{1,5},{2,6},{3,7},{4,0},{5,1},{6,2},{7,3},{8,12},{9,13},{10,... | collective-permute-start | bytes 24584 | tf_op jit(solution)/shard_map/ppermute | solution.py:13
  40.0 2.8 %copy-start.2 = (bf16[768,256]{1,0:T(8,128)(2,1)S(1)}, bf16[768,256]{1,0:T(8,128)(2,1)}, u32[]{:S(2)}) copy-start(bf16[768,256]{1,0:T(8,128)(2,1)} %param.28) | copy-start | bytes 1179652
  40.0 2.9 %copy-start.6 = (bf16[1,384,256]{2,1,0:T(8,128)(2,1)S(1)}, bf16[1,384,256]{2,1,0:T(8,128)(2,1)}, u32[]{:S(2)}) copy-start(bf16[1,384,256]{2,1,0:T(8,128)(2,1)} %param.18) | copy-start | bytes 589828
  43.2 20.8 %copy-start.9 = (f32[384,256]{1,0:T(8,128)}, f32[384,256]{1,0:T(8,128)S(1)}, u32[]{:S(2)}) copy-start(f32[384,256]{1,0:T(8,128)S(1)} %fusion.6) | copy-start | bytes 1179652
  46.8 72.5 %collective-permute-start.5 = (s32[64]{0:T(128)S(1)}, s32[64]{0:T(128)S(1)}, u32[]{:S(2)}, u32[]{:S(2)}) collective-permute-start(s32[64]{0:T(128)S(1)} %get-tuple-element.24), channel_id=1, source_target_pairs={{0,128},{128,0},{256,384},{384,256},{512,640},{640,512},{768,896},... | collective-permute-start | bytes 776 | tf_op jit(solution)/shard_map/ppermute | solution.py:13
  49.6 69.8 %collective-permute-start.7 = (s32[64]{0:T(128)S(1)}, s32[64]{0:T(128)S(1)}, u32[]{:S(2)}, u32[]{:S(2)}) collective-permute-start(s32[64]{0:T(128)S(1)} %get-tuple-element.25), channel_id=1, source_target_pairs={{0,256},{128,384},{256,0},{384,128},{512,768},{640,896},{768,512},... | collective-permute-start | bytes 776 | tf_op jit(solution)/shard_map/ppermute | solution.py:13
  54.1 65.5 %collective-permute-start.9 = (s32[64]{0:T(128)S(1)}, s32[64]{0:T(128)S(1)}, u32[]{:S(2)}, u32[]{:S(2)}) collective-permute-start(s32[64]{0:T(128)S(1)} %get-tuple-element.26), channel_id=1, source_target_pairs={{0,1},{1,0},{2,3},{3,2},{4,5},{5,4},{6,7},{7,6},{8,9},{9,8},{10,11... | collective-permute-start | bytes 776 | tf_op jit(solution)/shard_map/ppermute | solution.py:13
  56.9 7.2 %copy-start.8 = (bf16[256,256]{1,0:T(8,128)(2,1)S(1)}, bf16[256,256]{1,0:T(8,128)(2,1)}, u32[]{:S(2)}) copy-start(bf16[256,256]{1,0:T(8,128)(2,1)} %param.29) | copy-start | bytes 393220
  57.0 62.8 %collective-permute-start.11 = (s32[64]{0:T(128)S(1)}, s32[64]{0:T(128)S(1)}, u32[]{:S(2)}, u32[]{:S(2)}) collective-permute-start(s32[64]{0:T(128)S(1)} %get-tuple-element.27), channel_id=1, source_target_pairs={{0,2},{1,3},{2,0},{3,1},{4,6},{5,7},{6,4},{7,5},{8,10},{9,11},{10,... | collective-permute-start | bytes 776 | tf_op jit(solution)/shard_map/ppermute | solution.py:13
  64.5 7.3 %copy-start.7 = (bf16[256,256]{1,0:T(8,128)(2,1)S(1)}, bf16[256,256]{1,0:T(8,128)(2,1)}, u32[]{:S(2)}) copy-start(bf16[256,256]{1,0:T(8,128)(2,1)} %param.32) | copy-start | bytes 393220
  64.9 7.4 %copy-start.3 = (bf16[1,128,256]{2,1,0:T(8,128)(2,1)S(1)}, bf16[1,128,256]{2,1,0:T(8,128)(2,1)}, u32[]{:S(2)}) copy-start(bf16[1,128,256]{2,1,0:T(8,128)(2,1)} %param.20) | copy-start | bytes 196612
  64.9 7.4 %copy-start.5 = (f32[256]{0:T(256)S(1)}, f32[256]{0:T(256)}, u32[]{:S(2)}) copy-start(f32[256]{0:T(256)} %param.33) | copy-start | bytes 3076
  78.2 11.7 %collective-permute-start.6 = (bf16[64,256]{1,0:T(8,128)(2,1)S(1)}, bf16[64,256]{1,0:T(8,128)(2,1)S(1)}, u32[]{:S(2)}, u32[]{:S(2)}) collective-permute-start(bf16[64,256]{1,0:T(8,128)(2,1)S(1)} %get-tuple-element.14), channel_id=1, source_target_pairs={{0,128},{128,0},{256,384},{384,256},{512,640},{640,512},{768,896},... | collective-permute-start | bytes 98312 | tf_op jit(solution)/shard_map/ppermute | solution.py:13
  89.9 5.8 %collective-permute-start.8 = (bf16[64,256]{1,0:T(8,128)(2,1)S(1)}, bf16[64,256]{1,0:T(8,128)(2,1)S(1)}, u32[]{:S(2)}, u32[]{:S(2)}) collective-permute-start(bf16[64,256]{1,0:T(8,128)(2,1)S(1)} %get-tuple-element.13), channel_id=1, source_target_pairs={{0,256},{128,384},{256,0},{384,128},{512,768},{640,896},{768,512},... | collective-permute-start | bytes 98312 | tf_op jit(solution)/shard_map/ppermute | solution.py:13
  95.7 6.4 %collective-permute-start.10 = (bf16[64,256]{1,0:T(8,128)(2,1)S(1)}, bf16[64,256]{1,0:T(8,128)(2,1)S(1)}, u32[]{:S(2)}, u32[]{:S(2)}) collective-permute-start(bf16[64,256]{1,0:T(8,128)(2,1)S(1)} %get-tuple-element.12), channel_id=1, source_target_pairs={{0,1},{1,0},{2,3},{3,2},{4,5},{5,4},{6,7},{7,6},{8,9},{9,8},{10,11... | collective-permute-start | bytes 98312 | tf_op jit(solution)/shard_map/ppermute | solution.py:13
  102.1 7.3 %collective-permute-start.12 = (bf16[64,256]{1,0:T(8,128)(2,1)S(1)}, bf16[64,256]{1,0:T(8,128)(2,1)S(1)}, u32[]{:S(2)}, u32[]{:S(2)}) collective-permute-start(bf16[64,256]{1,0:T(8,128)(2,1)S(1)} %get-tuple-element.11), channel_id=1, source_target_pairs={{0,2},{1,3},{2,0},{3,1},{4,6},{5,7},{6,4},{7,5},{8,10},{9,11},{10,... | collective-permute-start | bytes 98312 | tf_op jit(solution)/shard_map/ppermute | solution.py:13
  109.4 5.8 %collective-permute-start.14 = (bf16[64,256]{1,0:T(8,128)(2,1)S(1)}, bf16[64,256]{1,0:T(8,128)(2,1)S(1)}, u32[]{:S(2)}, u32[]{:S(2)}) collective-permute-start(bf16[64,256]{1,0:T(8,128)(2,1)S(1)} %get-tuple-element.10), channel_id=1, source_target_pairs={{0,4},{1,5},{2,6},{3,7},{4,0},{5,1},{6,2},{7,3},{8,12},{9,13},{10,... | collective-permute-start | bytes 98312 | tf_op jit(solution)/shard_map/ppermute | solution.py:13
  115.2 7.8 %collective-permute-start.13 = (s32[64]{0:T(128)S(1)}, s32[64]{0:T(128)S(1)}, u32[]{:S(2)}, u32[]{:S(2)}) collective-permute-start(s32[64]{0:T(128)S(1)} %get-tuple-element.23), channel_id=1, source_target_pairs={{0,4},{1,5},{2,6},{3,7},{4,0},{5,1},{6,2},{7,3},{8,12},{9,13},{10,... | collective-permute-start | bytes 776 | tf_op jit(solution)/shard_map/ppermute | solution.py:13
  (2 other events, 1.8 us)
where the time goes:
time: 126 us; the launch traced here: 125 us
  starting transfers between devices  54.3 us (43%)
  other arithmetic  26.3 us (21%)
  local copies, waits for them, and re-layouts  24 us (19%)
  waiting for transfers between devices  12.2 us (10%)
  matrix products  4.97 us (4%)
  between operations  2.74 us (2%)
    ppermute x15, starting transfers between devices, partner(): lax.ppermute(shard, axis, [(i, i ^ 1 << apart) for i in range(lax.axis_si...  54.3 us
    ppermute x15, waiting for transfers between devices, partner(): lax.ppermute(shard, axis, [(i, i ^ 1 << apart) for i in range(lax.axis_si...  12.2 us
    gather x5, local copies, waits for them, and re-layouts, shards(): outgoing = nodes[boundary[round_index]]  7.13 us
    scatter-add x1, other arithmetic, shards(): jnp.zeros((node_rows, width), jnp.float32).at[receivers].add(message)  6.69 us
    scatter-add x5, other arithmetic, shards(): gradient.at[boundary[round_index]]  3.82 us
    gather x5, local copies, waits for them, and re-layouts, shards(): arrived[slots[round_index]]  3.5 us
    gather x5, local copies, waits for them, and re-layouts, shards(): nodes[cut_targets[round_index]]  3.5 us
    scatter-add x1, other arithmetic, shards(): gradient = gradient.at[receivers_local].add(local_grad[:, :width])  2.91 us
  transfers between devices with their start and end apart: 15, of which 4 were waited for; matrix products, arithmetic and copies ran while one was open for 41% of the time, Pallas kernels for 0%

commit v1 on v0

v1 whole, which is shorter than its diff:
```python
import jax
import jax.numpy as jnp
from jax import lax
from jax.experimental import pallas as pl
from jax.experimental.pallas import tpu as pltpu
from jax.sharding import PartitionSpec as P

F32 = jnp.float32
BF16 = jnp.bfloat16
MESH = pl.DeviceIdType.MESH
EPS = 1e-5

N = 128
L = 256
E = 384
R = 5
C = 64
S = 16
CUTS = R * C
ROWS = E + CUTS


def dot(a, b):
    return jnp.dot(a, b, preferred_element_type=F32)


def dot_nt(a, b):
    return lax.dot_general(a, b, (((1,), (1,)), ((), ())), preferred_element_type=F32)


def dot_tn(a, b):
    return lax.dot_general(a, b, (((0,), (0,)), ((), ())), preferred_element_type=F32)


def flip(index, bit):
    step = 1 << bit
    return index + step - 2 * step * lax.rem(lax.div(index, step), 2)


def column(rows_of, count, width):
    wide = jnp.concatenate([jnp.broadcast_to(rows_of(i), (width, width)) for i in range(count)], 0)
    total = count * width
    at = lax.broadcasted_iota(jnp.int32, (total, width), 0)
    lane = lax.broadcasted_iota(jnp.int32, (total, width), 1)
    keep = lax.rem(at, width) == lane
    return jnp.sum(jnp.where(keep, wide.astype(F32), 0.0), axis=1, keepdims=True)


def one_hot(col, width=N):
    lane = lax.broadcasted_iota(jnp.int32, (col.shape[0], width), 1).astype(F32)
    return (col == lane).astype(F32).astype(BF16)


def silu_pair(v):
    s = 0.5 * jnp.tanh(0.5 * v) + 0.5
    act = v * s
    return act, s + act * (1.0 - s)


def normed(y):
    mean = jnp.mean(y, axis=-1, keepdims=True)
    cent = y - mean
    var = jnp.mean(cent * cent, axis=-1, keepdims=True)
    inv = lax.rsqrt(var + EPS)
    return cent * inv, inv


def norm_back(d, xhat, inv):
    m1 = jnp.mean(d, axis=-1, keepdims=True)
    m2 = jnp.mean(d * xhat, axis=-1, keepdims=True)
    return inv * (d - m1 - xhat * m2)


def kernel(
    nodes_h, edges_h, cut_h, cot_h, send_h, recv_h, bound_h, slot_h, crecv_h, ncount_h, ecount_h,
    ef_h, es_h, eg_h, nf_h, ns_h, ng_h,
    upd_h, grad_h, egrad_h, cgrad_h,
    nodes, edges, cut, cot, sendi, recvi, bound, slot, crecv, ncount, ecount,
    ef, es, eg, nf, ns, ng,
    upd, grad, egrad, cgrad,
    out_rows, in_rows, out_sums, in_sums, comb, comb_cut, oh, oh2, xhat, inv, slope, gpe,
    in_sem, out_sem, s1, r1, s2, r2,
):
    g = lax.axis_index("grp")
    d = lax.axis_index("dev")
    partners = [
        (flip(g, 0), d), (flip(g, 1), d), (g, flip(d, 0)), (g, flip(d, 1)), (g, flip(d, 2)),
    ]
    barrier = pltpu.get_barrier_semaphore()
    for p in partners:
        pl.semaphore_signal(barrier, inc=1, device_id=p, device_id_type=MESH)

    pairs = [
        (nodes_h, nodes), (bound_h, bound), (recv_h, recvi), (send_h, sendi), (ecount_h, ecount),
        (ef_h, ef), (edges_h, edges), (es_h, es), (crecv_h, crecv), (slot_h, slot), (cut_h, cut),
        (nf_h, nf), (ns_h, ns), (eg_h, eg), (ng_h, ng), (cot_h, cot), (ncount_h, ncount),
    ]
    loads = {}
    for i, (src, dst) in enumerate(pairs):
        c = pltpu.make_async_copy(src, dst, in_sem.at[i])
        c.start()
        loads[id(dst)] = c

    def need(*refs):
        for r in refs:
            loads[id(r)].wait()

    in_rows[R * S:, :] = jnp.zeros((N - R * S, L), BF16)
    in_sums[R * S:, :] = jnp.zeros((N - R * S, L), BF16)

    need(nodes, bound)
    bcol = column(lambda i: bound[i:i + 1, :], R, S)
    ohb = one_hot(bcol)
    out_rows[...] = dot(ohb, nodes[...]).astype(BF16)
    pl.semaphore_wait(barrier, R)
    first = []
    for r, p in enumerate(partners):
        c = pltpu.make_async_remote_copy(
            src_ref=out_rows.at[pl.ds(S * r, S)], dst_ref=in_rows.at[pl.ds(S * r, S)],
            send_sem=s1.at[r], recv_sem=r1.at[r], device_id=p, device_id_type=MESH)
        c.start()
        first.append(c)

    need(recvi, sendi, ecount)
    rcol = column(lambda i: recvi[:, N * i:N * i + N], E // N, N)
    at = lax.broadcasted_iota(jnp.int32, (E, 1), 0)
    rcol = jnp.where(at < ecount[...], rcol, -1.0)
    oh[0:E, :] = one_hot(rcol)
    oh2[0:E, :] = one_hot(column(lambda i: sendi[:, N * i:N * i + N], E // N, N))

    need(ef)
    nr = dot(nodes[...], ef[0:L, :]).astype(BF16)
    comb[0:N, :] = nr
    comb[N:, :] = dot(nodes[...], ef[L:2 * L, :]).astype(BF16)
    comb_cut[0:N, :] = nr
    need(edges, es)

    def forward(start, size, latent, table):
        rows = pl.ds(start, size)
        pick = jnp.concatenate([oh[rows, :], oh2[rows, :]], 1)
        pre = dot(pick, table[...]) + dot(latent, ef[2 * L:, :])
        act, sl = silu_pair(pre)
        slope[rows, :] = sl
        xh, iv = normed(dot(act.astype(BF16), es[...]))
        xhat[rows, :] = xh.astype(BF16)
        inv[rows, :] = iv

    for b in range(E // 128):
        forward(128 * b, 128, edges[128 * b:128 * b + 128, :], comb)

    need(crecv, slot, cut, nf, ns, eg, ng, cot, ncount)
    oh[E:, :] = one_hot(column(lambda i: crecv[i:i + 1, :], R, C))
    rnd = lax.div(lax.broadcasted_iota(jnp.int32, (CUTS, 1), 0), C).astype(F32)
    oh2[E:, :] = one_hot(column(lambda i: slot[i:i + 1, :], R, C) + S * rnd)
    pre_node_own = dot(nodes[...], nf[0:L, :])

    for c in first:
        c.wait_recv()
    comb_cut[N:, :] = dot(in_rows[...], ef[L:2 * L, :]).astype(BF16)
    for b in range(2):
        forward(E + 160 * b, 160, cut[160 * b:160 * b + 160, :], comb_cut)

    received = (dot_tn(oh[...], xhat[...]) * eg[...]).astype(BF16)
    act, sl = silu_pair(pre_node_own + dot(received, nf[L:, :]))
    nx, ninv = normed(dot(act.astype(BF16), ns[...]))
    live = lax.broadcasted_iota(jnp.int32, (N, 1), 0) < ncount[...]
    gain = ng[...]
    upd[...] = jnp.where(live, nodes[...].astype(F32) + nx * gain, 0.0).astype(BF16)
    out0 = pltpu.make_async_copy(upd, upd_h, out_sem.at[0])
    out0.start()
    mcot = jnp.where(live, cot[...].astype(F32), 0.0)
    goo = norm_back(mcot * gain, nx, ninv).astype(BF16)
    gpn = (dot_nt(goo, ns[...]) * sl).astype(BF16)
    base = mcot + dot_nt(gpn, nf[0:L, :])
    gm = (dot_nt(gpn, nf[L:, :]) * eg[...]).astype(BF16)

    def backward(start, size):
        rows = pl.ds(start, size)
        dd = dot(oh[rows, :], gm)
        goe = norm_back(dd, xhat[rows, :].astype(F32), inv[rows, :]).astype(BF16)
        gpe[rows, :] = (dot_nt(goe, es[...]) * slope[rows, :]).astype(BF16)

    for b in range(2):
        backward(E + 160 * b, 160)
    out_sums[...] = dot_tn(oh2[E:, :], gpe[E:, :]).astype(BF16)
    second = []
    for r, p in enumerate(partners):
        c = pltpu.make_async_remote_copy(
            src_ref=out_sums.at[pl.ds(S * r, S)], dst_ref=in_sums.at[pl.ds(S * r, S)],
            send_sem=s2.at[r], recv_sem=r2.at[r], device_id=p, device_id_type=MESH)
        c.start()
        second.append(c)
    cgrad[...] = dot_nt(gpe[E:, :], ef[2 * L:, :]).astype(BF16)
    out3 = pltpu.make_async_copy(cgrad, cgrad_h, out_sem.at[3])
    out3.start()
    for b in range(E // 128):
        backward(128 * b, 128)
    egrad[...] = dot_nt(gpe[0:E, :], ef[2 * L:, :]).astype(BF16)
    out2 = pltpu.make_async_copy(egrad, egrad_h, out_sem.at[2])
    out2.start()
    rsum = dot_tn(oh[...], gpe[...]).astype(BF16)
    base = base + dot_nt(rsum, ef[0:L, :])
    ssum = dot_tn(oh2[0:E, :], gpe[0:E, :])
    for c in second:
        c.wait_recv()
    ssum = (ssum + dot_tn(ohb, in_sums[0:R * S, :])).astype(BF16)
    grad[...] = (base + dot_nt(ssum, ef[L:2 * L, :])).astype(BF16)
    out1 = pltpu.make_async_copy(grad, grad_h, out_sem.at[1])
    out1.start()
    for c in first + second:
        c.wait_send()
    for c in (out0, out1, out2, out3):
        c.wait()


def shards(
    node_latent, edge_latent, cut_latent, node_cotangent, edge_sender, edge_receiver, boundary_rows,
    cut_slot, cut_receiver, node_count, edge_count, edge_first, edge_second, edge_gain, node_first,
    node_second, node_gain,
):
    i32 = jnp.int32
    anyspec = pl.BlockSpec(memory_space=pl.ANY)
    outs = pl.pallas_call(
        kernel,
        out_shape=(
            jax.ShapeDtypeStruct((N, L), BF16),
            jax.ShapeDtypeStruct((N, L), BF16),
            jax.ShapeDtypeStruct((E, L), BF16),
            jax.ShapeDtypeStruct((CUTS, L), BF16),
        ),
        in_specs=[anyspec] * 17,
        out_specs=(anyspec,) * 4,
        scratch_shapes=[
            pltpu.VMEM((N, L), BF16), pltpu.VMEM((E, L), BF16), pltpu.VMEM((CUTS, L), BF16),
            pltpu.VMEM((N, L), BF16), pltpu.VMEM((1, E), i32), pltpu.VMEM((1, E), i32),
            pltpu.VMEM((R, S), i32), pltpu.VMEM((R, C), i32), pltpu.VMEM((R, C), i32),
            pltpu.VMEM((1, 1), i32), pltpu.VMEM((1, 1), i32),
            pltpu.VMEM((3 * L, L), BF16), pltpu.VMEM((L, L), BF16), pltpu.VMEM((1, L), F32),
            pltpu.VMEM((2 * L, L), BF16), pltpu.VMEM((L, L), BF16), pltpu.VMEM((1, L), F32),
            pltpu.VMEM((N, L), BF16), pltpu.VMEM((N, L), BF16), pltpu.VMEM((E, L), BF16),
            pltpu.VMEM((CUTS, L), BF16),
            pltpu.VMEM((R * S, L), BF16), pltpu.VMEM((N, L), BF16),
            pltpu.VMEM((N, L), BF16), pltpu.VMEM((N, L), BF16),
            pltpu.VMEM((2 * N, L), BF16), pltpu.VMEM((2 * N, L), BF16),
            pltpu.VMEM((ROWS, N), BF16), pltpu.VMEM((ROWS, N), BF16),
            pltpu.VMEM((ROWS, L), BF16), pltpu.VMEM((ROWS, 1), F32), pltpu.VMEM((ROWS, L), F32),
            pltpu.VMEM((ROWS, L), BF16),
            pltpu.SemaphoreType.DMA((17,)), pltpu.SemaphoreType.DMA((4,)),
            pltpu.SemaphoreType.DMA((R,)), pltpu.SemaphoreType.DMA((R,)),
            pltpu.SemaphoreType.DMA((R,)), pltpu.SemaphoreType.DMA((R,)),
        ],
        compiler_params=pltpu.CompilerParams(collective_id=0, has_side_effects=True),
        name="message_step",
    )(
        node_latent[0], edge_latent[0], cut_latent[0].reshape(CUTS, L), node_cotangent[0],
        edge_sender, edge_receiver, boundary_rows[0], cut_slot[0], cut_receiver[0],
        node_count.reshape(1, 1), edge_count.reshape(1, 1),
        edge_first, edge_second, edge_gain.reshape(1, L), node_first, node_second,
        node_gain.reshape(1, L),
    )
    updated, gradient, edge_gradient, cut_gradient = outs
    return updated[None], gradient[None], edge_gradient[None], cut_gradient.reshape(1, R, C, L)


def solution(mesh):
    part = ("grp", "dev")
    three = P(part, None, None)
    four = P(part, None, None, None)
    placed = (
        three, three, four, three, P(part, None), P(part, None), three, three, three, P(part),
        P(part), P(), P(), P(), P(), P(), P(),
    )
    return jax.shard_map(
        shards, mesh=mesh, in_specs=placed, out_specs=(three, three, three, four), check_vma=False,
    )
```

time: 126 us -> 33.6 us (0.27)
  the two profiles are of different devices: /device:TPU:8 before, /device:TPU:2 now
where the time goes in v1:
time: 33.6 us; the launch traced here: 33.3 us
  Pallas kernels  24.7 us (74%)
  local copies, waits for them, and re-layouts  6.62 us (20%)
  between operations  1.96 us (6%)
    pallas_call x1, Pallas kernels, shards(): pl.pallas_call(kernel, out_shape=(jax.ShapeDtypeStruct((N, L), BF16), jax...  24.7 us
    unnamed x16, local copies, waits for them, and re-layouts  6.62 us

profile of v1, /device:TPU:2, one launch (start us, length us, event | category | flops | bytes accessed | tf_op | source)
XLA Modules:
  0.0 33.3 jit_solution(12743982928805122524)
XLA Ops:
  1.9 0.0 copy-start.2
  1.9 0.7 %copy-done.2 = s32[1,5,16]{2,0,1:T(1,128)S(1)} copy-done((s32[1,5,16]{2,0,1:T(1,128)S(1)}, s32[1,5,16]{2,0,1:T(1,128)}, u32[]{:S(2)}) %copy-start.2) | copy-done | bytes 344
  2.6 0.0 copy-start.3
  2.6 0.0 copy-start.4
  2.6 0.6 %copy.27 = s32[1,5,16]{2,1,0:T(8,128)} copy(s32[1,5,16]{2,0,1:T(1,128)S(1)} %copy-done.2) | data formatting | bytes 640
  3.2 0.1 copy-done.3
  3.3 0.0 copy-done.4
  3.3 0.6 %copy_bitcast_fusion = (s32[5,64]{1,0:T(8,128)}, s32[5,64]{1,0:T(8,128)}) fusion(s32[1,5,64]{2,0,1:T(1,128)S(1)} %copy-done.3, s32[1,5,64]{2,0,1:T(1,128)S(1)} %copy-done.4), kind=kLoop, calls=%fused_computation | loop fusion | bytes 5120
  3.9 24.7 %message_step.1 = (bf16[128,256]{1,0:T(8,128)(2,1)}, bf16[128,256]{1,0:T(8,128)(2,1)}, bf16[384,256]{1,0:T(8,128)(2,1)}, bf16[320,256]{1,0:T(8,128)(2,1)}) custom-call(bf16[128,256]{1,0:T(8,128)(2,1)} %bitcast.25, bf16[384,256]{1,0:T(8,128)(2,1)} %bitcast.22, bf16[320,256]{1,0:T(8,128)(2,1)} %bitcast.24, bf16[128,256]{1,0:T(8,128)(2,1)} %bitcast.26, ...), custom_call_target="tpu_custom_call" | custom-call | tf_op jit(solution)/shard_map/message_step/pallas_call | solution.py:223
  28.6 0.0 copy-start
  28.7 1.5 %copy.34 = bf16[1,128,256]{2,1,0:T(8,128)(2,1)} copy(bf16[1,128,256]{2,1,0:T(8,128)(2,1)} %bitcast.28) | data formatting | bytes 131072
  30.2 1.5 %copy.35 = bf16[1,128,256]{2,1,0:T(8,128)(2,1)} copy(bf16[1,128,256]{2,1,0:T(8,128)(2,1)} %bitcast.27) | data formatting | bytes 131072
  31.6 0.0 copy-done
  31.6 0.0 copy-start.1
  31.6 0.7 %copy.36 = bf16[1,384,256]{2,1,0:T(8,128)(2,1)} copy(bf16[1,384,256]{2,1,0:T(8,128)(2,1)S(1)} %bitcast.21) | data formatting | bytes 393216
  32.3 0.3 copy-done.1
  32.6 0.7 %copy.37 = bf16[1,5,64,256]{3,2,1,0:T(8,128)(2,1)} copy(bf16[1,5,64,256]{3,2,1,0:T(8,128)(2,1)S(1)} %bitcast.23) | data formatting | bytes 327680
Async XLA Ops:
  1.9 0.7 %copy-start.2 = (s32[1,5,16]{2,0,1:T(1,128)S(1)}, s32[1,5,16]{2,0,1:T(1,128)}, u32[]{:S(2)}) copy-start(s32[1,5,16]{2,0,1:T(1,128)} %param.23) | copy-start | bytes 964
  2.6 0.7 %copy-start.3 = (s32[1,5,64]{2,0,1:T(1,128)S(1)}, s32[1,5,64]{2,0,1:T(1,128)}, u32[]{:S(2)}) copy-start(s32[1,5,64]{2,0,1:T(1,128)} %param.25) | copy-start | bytes 3844
  2.6 0.7 %copy-start.4 = (s32[1,5,64]{2,0,1:T(1,128)S(1)}, s32[1,5,64]{2,0,1:T(1,128)}, u32[]{:S(2)}) copy-start(s32[1,5,64]{2,0,1:T(1,128)} %param.24) | copy-start | bytes 3844
  28.6 3.0 %copy-start = (bf16[384,256]{1,0:T(8,128)(2,1)S(1)}, bf16[384,256]{1,0:T(8,128)(2,1)}, u32[]{:S(2)}) copy-start(bf16[384,256]{1,0:T(8,128)(2,1)} %get-tuple-element.10) | copy-start | bytes 589828
  31.6 1.0 %copy-start.1 = (bf16[320,256]{1,0:T(8,128)(2,1)S(1)}, bf16[320,256]{1,0:T(8,128)(2,1)}, u32[]{:S(2)}) copy-start(bf16[320,256]{1,0:T(8,128)(2,1)} %get-tuple-element.11) | copy-start | bytes 491524

commit v2 on v1

--- a/solution.py
+++ b/solution.py
@@ -74,12 +74,11 @@
 def kernel(
     nodes_h, edges_h, cut_h, cot_h, send_h, recv_h, bound_h, slot_h, crecv_h, ncount_h, ecount_h,
     ef_h, es_h, eg_h, nf_h, ns_h, ng_h,
-    upd_h, grad_h, egrad_h, cgrad_h,
+    upd, grad, egrad, cgrad,
     nodes, edges, cut, cot, sendi, recvi, bound, slot, crecv, ncount, ecount,
     ef, es, eg, nf, ns, ng,
-    upd, grad, egrad, cgrad,
     out_rows, in_rows, out_sums, in_sums, comb, comb_cut, oh, oh2, xhat, inv, slope, gpe,
-    in_sem, out_sem, s1, r1, s2, r2,
+    in_sem, s1, r1, s2, r2,
 ):
     g = lax.axis_index("grp")
     d = lax.axis_index("dev")
@@ -109,7 +108,7 @@
     in_sums[R * S:, :] = jnp.zeros((N - R * S, L), BF16)
 
     need(nodes, bound)
-    bcol = column(lambda i: bound[i:i + 1, :], R, S)
+    bcol = column(lambda i: bound[i], R, S)
     ohb = one_hot(bcol)
     out_rows[...] = dot(ohb, nodes[...]).astype(BF16)
     pl.semaphore_wait(barrier, R)
@@ -149,9 +148,9 @@
         forward(128 * b, 128, edges[128 * b:128 * b + 128, :], comb)
 
     need(crecv, slot, cut, nf, ns, eg, ng, cot, ncount)
-    oh[E:, :] = one_hot(column(lambda i: crecv[i:i + 1, :], R, C))
+    oh[E:, :] = one_hot(column(lambda i: crecv[i], R, C))
     rnd = lax.div(lax.broadcasted_iota(jnp.int32, (CUTS, 1), 0), C).astype(F32)
-    oh2[E:, :] = one_hot(column(lambda i: slot[i:i + 1, :], R, C) + S * rnd)
+    oh2[E:, :] = one_hot(column(lambda i: slot[i], R, C) + S * rnd)
     pre_node_own = dot(nodes[...], nf[0:L, :])
 
     for c in first:
@@ -166,8 +165,6 @@
     live = lax.broadcasted_iota(jnp.int32, (N, 1), 0) < ncount[...]
     gain = ng[...]
     upd[...] = jnp.where(live, nodes[...].astype(F32) + nx * gain, 0.0).astype(BF16)
-    out0 = pltpu.make_async_copy(upd, upd_h, out_sem.at[0])
-    out0.start()
     mcot = jnp.where(live, cot[...].astype(F32), 0.0)
     goo = norm_back(mcot * gain, nx, ninv).astype(BF16)
     gpn = (dot_nt(goo, ns[...]) * sl).astype(BF16)
@@ -191,13 +188,9 @@
         c.start()
         second.append(c)
     cgrad[...] = dot_nt(gpe[E:, :], ef[2 * L:, :]).astype(BF16)
-    out3 = pltpu.make_async_copy(cgrad, cgrad_h, out_sem.at[3])
-    out3.start()
     for b in range(E // 128):
         backward(128 * b, 128)
     egrad[...] = dot_nt(gpe[0:E, :], ef[2 * L:, :]).astype(BF16)
-    out2 = pltpu.make_async_copy(egrad, egrad_h, out_sem.at[2])
-    out2.start()
     rsum = dot_tn(oh[...], gpe[...]).astype(BF16)
     base = base + dot_nt(rsum, ef[0:L, :])
     ssum = dot_tn(oh2[0:E, :], gpe[0:E, :])
@@ -205,12 +198,19 @@
         c.wait_recv()
     ssum = (ssum + dot_tn(ohb, in_sums[0:R * S, :])).astype(BF16)
     grad[...] = (base + dot_nt(ssum, ef[L:2 * L, :])).astype(BF16)
-    out1 = pltpu.make_async_copy(grad, grad_h, out_sem.at[1])
-    out1.start()
     for c in first + second:
         c.wait_send()
-    for c in (out0, out1, out2, out3):
-        c.wait()
+
+
+def write_out(a, b, c, e, a_h, b_h, c_h, e_h, sem):
+    copies = [
+        pltpu.make_async_copy(src, dst, sem.at[i])
+        for i, (src, dst) in enumerate(((a, a_h), (b, b_h), (c, c_h), (e, e_h)))
+    ]
+    for copy in copies:
+        copy.start()
+    for copy in copies:
+        copy.wait()
 
 
 def shards(
@@ -222,30 +222,23 @@
     anyspec = pl.BlockSpec(memory_space=pl.ANY)
     outs = pl.pallas_call(
         kernel,
-        out_shape=(
-            jax.ShapeDtypeStruct((N, L), BF16),
-            jax.ShapeDtypeStruct((N, L), BF16),
-            jax.ShapeDtypeStruct((E, L), BF16),
-            jax.ShapeDtypeStruct((CUTS, L), BF16),
-        ),
+        out_shape=tuple(pltpu.VMEM((n, L), BF16) for n in (N, N, E, CUTS)),
         in_specs=[anyspec] * 17,
-        out_specs=(anyspec,) * 4,
+        out_specs=(pl.BlockSpec(memory_space=pltpu.VMEM),) * 4,
         scratch_shapes=[
             pltpu.VMEM((N, L), BF16), pltpu.VMEM((E, L), BF16), pltpu.VMEM((CUTS, L), BF16),
             pltpu.VMEM((N, L), BF16), pltpu.VMEM((1, E), i32), pltpu.VMEM((1, E), i32),
-            pltpu.VMEM((R, S), i32), pltpu.VMEM((R, C), i32), pltpu.VMEM((R, C), i32),
+            pltpu.VMEM((R, 1, S), i32), pltpu.VMEM((R, 1, C), i32), pltpu.VMEM((R, 1, C), i32),
             pltpu.VMEM((1, 1), i32), pltpu.VMEM((1, 1), i32),
             pltpu.VMEM((3 * L, L), BF16), pltpu.VMEM((L, L), BF16), pltpu.VMEM((1, L), F32),
             pltpu.VMEM((2 * L, L), BF16), pltpu.VMEM((L, L), BF16), pltpu.VMEM((1, L), F32),
-            pltpu.VMEM((N, L), BF16), pltpu.VMEM((N, L), BF16), pltpu.VMEM((E, L), BF16),
-            pltpu.VMEM((CUTS, L), BF16),
             pltpu.VMEM((R * S, L), BF16), pltpu.VMEM((N, L), BF16),
             pltpu.VMEM((N, L), BF16), pltpu.VMEM((N, L), BF16),
             pltpu.VMEM((2 * N, L), BF16), pltpu.VMEM((2 * N, L), BF16),
             pltpu.VMEM((ROWS, N), BF16), pltpu.VMEM((ROWS, N), BF16),
             pltpu.VMEM((ROWS, L), BF16), pltpu.VMEM((ROWS, 1), F32), pltpu.VMEM((ROWS, L), F32),
             pltpu.VMEM((ROWS, L), BF16),
-            pltpu.SemaphoreType.DMA((17,)), pltpu.SemaphoreType.DMA((4,)),
+            pltpu.SemaphoreType.DMA((17,)),
             pltpu.SemaphoreType.DMA((R,)), pltpu.SemaphoreType.DMA((R,)),
             pltpu.SemaphoreType.DMA((R,)), pltpu.SemaphoreType.DMA((R,)),
         ],
@@ -253,12 +246,19 @@
         name="message_step",
     )(
         node_latent[0], edge_latent[0], cut_latent[0].reshape(CUTS, L), node_cotangent[0],
-        edge_sender, edge_receiver, boundary_rows[0], cut_slot[0], cut_receiver[0],
+        edge_sender, edge_receiver, boundary_rows.reshape(R, 1, S), cut_slot.reshape(R, 1, C), cut_receiver.reshape(R, 1, C),
         node_count.reshape(1, 1), edge_count.reshape(1, 1),
         edge_first, edge_second, edge_gain.reshape(1, L), node_first, node_second,
         node_gain.reshape(1, L),
     )
-    updated, gradient, edge_gradient, cut_gradient = outs
+    updated, gradient, edge_gradient, cut_gradient = pl.pallas_call(
+        write_out,
+        out_shape=tuple(jax.ShapeDtypeStruct((n, L), BF16) for n in (N, N, E, CUTS)),
+        in_specs=[pl.BlockSpec(memory_space=pltpu.VMEM)] * 4,
+        out_specs=(anyspec,) * 4,
+        scratch_shapes=[pltpu.SemaphoreType.DMA((4,))],
+        name="write_out",
+    )(*(pltpu.with_memory_space_constraint(o, pltpu.VMEM) for o in outs))
     return updated[None], gradient[None], edge_gradient[None], cut_gradient.reshape(1, R, C, L)
 
 

time: 33.6 us -> 27 us (0.80)
  local copies, waits for them, and re-layouts: 6.62 us -> 0 us
    unnamed x16 -> x0, local copies, waits for them, and re-layouts: 6.62 us -> none
    pallas_call x1 -> x2, Pallas kernels: 24.7 us -> 24.9 us  [the longest x1 24.1 us: shards(): pl.pallas_call(kernel, out_shape=tuple((pltpu.VMEM((n, L), BF16) for n in...]
where the time goes in v2:
time: 27 us; the launch traced here: 26.8 us
  Pallas kernels  24.9 us (92%)
  between operations  1.94 us (7%)
    pallas_call x1, Pallas kernels, shards(): pl.pallas_call(kernel, out_shape=tuple((pltpu.VMEM((n, L), BF16) for n in...  24.1 us
    pallas_call x1, Pallas kernels, shards(): pl.pallas_call(write_out, out_shape=tuple((jax.ShapeDtypeStruct((n, L), B...  0.81 us

profile of v2, /device:TPU:2, one launch (start us, length us, event | category | flops | bytes accessed | tf_op | source)
XLA Modules:
  0.0 26.8 jit_solution(12327918486194275852)
XLA Ops:
  1.9 24.1 %message_step.1 = (bf16[128,256]{1,0:T(8,128)(2,1)S(1)}, bf16[128,256]{1,0:T(8,128)(2,1)S(1)}, bf16[384,256]{1,0:T(8,128)(2,1)S(1)}, bf16[320,256]{1,0:T(8,128)(2,1)S(1)}) custom-call(bf16[128,256]{1,0:T(8,128)(2,1)} %bitcast.19, bf16[384,256]{1,0:T(8,128)(2,1)} %bitcast.17, bf16[320,256]{1,0:T(8,128)(2,1)} %bitcast.18, bf16[128,256]{1,0:T(8,128)(2,1)} %bitcast.20, ...), custom_call_target="tpu_custom_call" | custom-call | tf_op jit(solution)/shard_map/message_step/pallas_call | solution.py:223
  26.0 0.8 %write_out.1 = (bf16[128,256]{1,0:T(8,128)(2,1)}, bf16[128,256]{1,0:T(8,128)(2,1)}, bf16[384,256]{1,0:T(8,128)(2,1)}, bf16[320,256]{1,0:T(8,128)(2,1)}) custom-call(bf16[128,256]{1,0:T(8,128)(2,1)S(1)} %get-tuple-element.12.a, bf16[128,256]{1,0:T(8,128)(2,1)S(1)} %get-tuple-element.13.b, bf16[384,256]{1,0:T(8,128)(2,1)S(1)} %get-tuple-element.14.c, ...), custom_call_target="tpu_custom_call" | custom-call | tf_op jit(solution)/shard_map/write_out/pallas_call | solution.py:254

commit v3 on v2

v3 whole, which is shorter than its diff:
```python
import jax
import jax.numpy as jnp
from jax import lax
from jax.experimental import pallas as pl
from jax.experimental.pallas import tpu as pltpu
from jax.sharding import PartitionSpec as P

F32 = jnp.float32
BF16 = jnp.bfloat16
MESH = pl.DeviceIdType.MESH
EPS = 1e-5

N = 128
L = 256
E = 384
R = 5
C = 64
S = 16
CUTS = R * C
ROWS = E + CUTS


def dot(a, b):
    return jnp.dot(a, b, preferred_element_type=F32)


def dot_nt(a, b):
    return lax.dot_general(a, b, (((1,), (1,)), ((), ())), preferred_element_type=F32)


def flip(index, bit):
    step = 1 << bit
    return index + step - 2 * step * lax.rem(lax.div(index, step), 2)


def column(rows_of, count, width):
    wide = jnp.concatenate([jnp.broadcast_to(rows_of(i), (width, width)) for i in range(count)], 0)
    total = count * width
    at = lax.broadcasted_iota(jnp.int32, (total, width), 0)
    lane = lax.broadcasted_iota(jnp.int32, (total, width), 1)
    keep = lax.rem(at, width) == lane
    return jnp.sum(jnp.where(keep, wide.astype(F32), 0.0), axis=1, keepdims=True)


def one_hot(col, width=N):
    lane = lax.broadcasted_iota(jnp.int32, (col.shape[0], width), 1).astype(F32)
    return (col == lane).astype(F32).astype(BF16)


def one_hot_t(row):
    at = lax.broadcasted_iota(jnp.int32, (N, row.shape[1]), 0)
    return (at == row).astype(F32).astype(BF16)


def silu_pair(half):
    t = jnp.tanh(half)
    act = half + half * t
    return act, (1.0 + t) + act * (1.0 - t)


def twice(a):
    return jnp.concatenate([a, a], 1)


def row_means(w):
    mean = dot_nt(jnp.full((N, L), 1.0 / L, BF16), w)
    high = mean.astype(BF16)
    return jnp.concatenate([high, (mean - high.astype(F32)).astype(BF16)], 1)


def centred(act, w, means):
    return dot(act, w) - twice(dot_nt(twice(act), means))


def total_of(a):
    return jnp.sum(a, axis=-1, keepdims=True)


def kernel(
    nodes_h, edges_h, cut_h, cot_h, send_h, recv_h, bound_h, slot_h, crecv_h, ncount_h, ecount_h,
    ef_h, es_h, eg_h, nf_h, ns_h, ng_h,
    upd, grad, egrad, cgrad,
    nodes, edges, cut, cot, sendi, recvi, bound, slot, crecv, ncount, ecount,
    ef, es, eg, nf, ns, ng,
    out_rows, in_rows, out_sums, in_sums, comb, weh, oht, pick, part, xb, side, slope, gpe,
    in_sem, s1, r1, s2, r2,
):
    loads = {}

    def load(key, src, dst):
        c = pltpu.make_async_copy(src, dst, in_sem.at[len(loads)])
        c.start()
        loads[key] = c

    def need(*keys):
        for k in keys:
            loads[k].wait()

    load("nodes", nodes_h, nodes)
    load("bound", bound_h, bound)
    g = lax.axis_index("grp")
    d = lax.axis_index("dev")
    partners = [
        (flip(g, 0), d), (flip(g, 1), d), (g, flip(d, 0)), (g, flip(d, 1)), (g, flip(d, 2)),
    ]
    barrier = pltpu.get_barrier_semaphore()
    for p in partners[::-1]:
        pl.semaphore_signal(barrier, inc=1, device_id=p, device_id_type=MESH)
    load("recv", recv_h, recvi)
    load("send", send_h, sendi)
    load("ecount", ecount_h, ecount)
    load("ef", ef_h, ef)
    load("edges", edges_h, edges)
    load("es", es_h, es)
    load("crecv", crecv_h, crecv)
    load("slot", slot_h, slot)
    load("cut", cut_h, cut)
    load("eg", eg_h, eg)
    load("nf", nf_h, nf)
    load("ns", ns_h, ns)
    load("ng", ng_h, ng)
    load("cot", cot_h, cot)
    load("ncount", ncount_h, ncount)

    eye = one_hot_t(lax.broadcasted_iota(jnp.int32, (1, N), 1))

    need("nodes", "bound")
    ohb = one_hot(column(lambda i: bound[i], R, S))
    out_rows[...] = dot(ohb, nodes[...]).astype(BF16)
    pl.semaphore_wait(barrier, R)

    def exchange(src, dst, send_sem, recv_sem):
        copies = []
        for r in (3, 1, 2, 4, 0):
            at = pl.ds(S * r, S)
            c = pltpu.make_async_remote_copy(
                src_ref=src.at[at], dst_ref=dst.at[at], send_sem=send_sem.at[r],
                recv_sem=recv_sem.at[r], device_id=partners[r], device_id_type=MESH)
            c.start()
            copies.append(c)
        return copies

    first = exchange(out_rows, in_rows, s1, r1)

    def tables(start, size):
        for b in range(start, start + size, N):
            n = min(N, start + size - b)
            pick[b:b + n, :] = dot_nt(eye[:n, :n], oht[:, b:b + n]).astype(BF16)

    def forward(start, half):
        size = half.shape[0]
        rows = pl.ds(start, size)
        act, sl = silu_pair(half)
        cent = centred(act.astype(BF16), es[...], edge_means)
        inv = lax.rsqrt(total_of(cent * cent) * (1.0 / L) + EPS)
        xh = (cent * inv).astype(BF16)
        xb[rows, :] = xh
        slope[rows, :] = sl * inv
        return dot(oht[0:N, start:start + size], xh)

    need("recv", "send", "ecount")
    lane = lax.broadcasted_iota(jnp.int32, (1, E), 1)
    oht[0:N, 0:E] = one_hot_t(jnp.where(lane < ecount[...], recvi[...], -1))
    oht[N:, 0:E] = one_hot_t(sendi[...])
    tables(0, E)
    need("ef")
    sender = ef[L:2 * L, :]
    weh[...] = (ef[2 * L:, :].astype(F32) * 0.5).astype(BF16)
    comb[0:N, :] = (dot(nodes[...], ef[0:L, :]) * 0.5).astype(BF16)
    comb[N:, :] = (dot(nodes[...], sender) * 0.5).astype(BF16)
    need("edges", "es")
    edge_means = row_means(es[...])
    total = forward(0, dot(pick[0:E, :], comb[...]) + dot(edges[...], weh[...]))

    need("crecv", "slot", "cut", "eg", "nf", "ns", "ng", "cot", "ncount")
    oht[0:N, E:] = one_hot_t(jnp.concatenate([crecv[r] for r in range(R)], 1))
    oht[N:, E:] = one_hot_t(jnp.concatenate([slot[r] + S * r for r in range(R)], 1))
    tables(E, CUTS)
    part[...] = dot(pick[E:, 0:N], comb[0:N, :]) + dot(cut[...], weh[...])
    ohtb = one_hot_t(jnp.concatenate([bound[r] for r in range(R)], 1))
    node_means = row_means(ns[...])
    pre_node_own = dot(nodes[...], nf[0:L, :])
    es_f = es[...].astype(F32)
    es_c = ((es_f - total_of(es_f) * (1.0 / L)) * (0.5 * eg[...])).astype(BF16)
    chain = dot(es_c, nf[L:, :]).astype(BF16)
    live = lax.broadcasted_iota(jnp.int32, (N, 1), 0) < ncount[...]
    gain = ng[...]
    mcot = jnp.where(live, cot[...].astype(F32), 0.0)
    dc = mcot * gain
    dc = dc - total_of(dc) * (1.0 / L)

    for c in first:
        c.wait_recv()
    arrived = (dot(in_rows[...], sender) * 0.5).astype(BF16)
    arrived = jnp.concatenate([arrived, jnp.zeros((N - R * S, L), BF16)], 0)
    total = total + forward(E, part[...] + dot(pick[E:, N:], arrived))

    received = (total * eg[...]).astype(BF16)
    act, sl = silu_pair(0.5 * (pre_node_own + dot(received, nf[L:, :])))
    cent = centred(act.astype(BF16), ns[...], node_means)
    along = total_of(dc * cent) * (1.0 / L)
    ninv = lax.rsqrt(total_of(cent * cent) * (1.0 / L) + EPS)
    goo = (ninv * dc - cent * (ninv * ninv * ninv * along)).astype(BF16)
    gpn = (dot_nt(goo, ns[...]) * (0.5 * sl)).astype(BF16)
    gm = (dot_nt(gpn, nf[L:, :]) * (0.5 * eg[...])).astype(BF16)
    gm2 = dot_nt(gpn, chain).astype(BF16)

    def backward(start, size):
        rows = pl.ds(start, size)
        to = pick[rows, 0:N]
        m2 = total_of(dot_nt(xb[rows, :], gm) * to.astype(F32)) * (1.0 / L)
        gpe[rows, :] = ((dot(to, gm2) - m2 * side[rows, :]) * slope[rows, :]).astype(BF16)

    side[E:, :] = dot_nt(xb[E:, :], es[...])
    backward(E, CUTS)
    out_sums[...] = dot(oht[N:N + R * S, E:], gpe[E:, :]).astype(BF16)
    second = exchange(out_sums, in_sums, s2, r2)

    upd[...] = jnp.where(live, nodes[...].astype(F32) + cent * ninv * gain, 0.0).astype(BF16)
    base = mcot + dot_nt(gpn, nf[0:L, :])
    latent_t = ef[2 * L:, :]
    cgrad[...] = dot_nt(gpe[E:, :], latent_t).astype(BF16)
    side[0:E, :] = dot_nt(xb[0:E, :], es[...])
    backward(0, E)
    egrad[...] = dot_nt(gpe[0:E, :], latent_t).astype(BF16)
    rsum = dot(oht[0:N, :], gpe[...]).astype(BF16)
    base = base + dot_nt(rsum, ef[0:L, :])
    ssum = dot(oht[N:, 0:E], gpe[0:E, :])
    for c in second:
        c.wait_recv()
    ssum = (ssum + dot(ohtb, in_sums[...])).astype(BF16)
    grad[...] = (base + dot_nt(ssum, sender)).astype(BF16)
    for c in first + second:
        c.wait_send()


def write_out(a, b, c, e, a_h, b_h, c_h, e_h, sem):
    copies = [
        pltpu.make_async_copy(src, dst, sem.at[i])
        for i, (src, dst) in enumerate(((a, a_h), (b, b_h), (c, c_h), (e, e_h)))
    ]
    for copy in copies:
        copy.start()
    for copy in copies:
        copy.wait()


def shards(
    node_latent, edge_latent, cut_latent, node_cotangent, edge_sender, edge_receiver, boundary_rows,
    cut_slot, cut_receiver, node_count, edge_count, edge_first, edge_second, edge_gain, node_first,
    node_second, node_gain,
):
    i32 = jnp.int32
    anyspec = pl.BlockSpec(memory_space=pl.ANY)
    outs = pl.pallas_call(
        kernel,
        out_shape=tuple(pltpu.VMEM((n, L), BF16) for n in (N, N, E, CUTS)),
        in_specs=[anyspec] * 17,
        out_specs=(pl.BlockSpec(memory_space=pltpu.VMEM),) * 4,
        scratch_shapes=[
            pltpu.VMEM((N, L), BF16), pltpu.VMEM((E, L), BF16), pltpu.VMEM((CUTS, L), BF16),
            pltpu.VMEM((N, L), BF16), pltpu.VMEM((1, E), i32), pltpu.VMEM((1, E), i32),
            pltpu.VMEM((R, 1, S), i32), pltpu.VMEM((R, 1, C), i32), pltpu.VMEM((R, 1, C), i32),
            pltpu.VMEM((1, 1), i32), pltpu.VMEM((1, 1), i32),
            pltpu.VMEM((3 * L, L), BF16), pltpu.VMEM((L, L), BF16), pltpu.VMEM((1, L), F32),
            pltpu.VMEM((2 * L, L), BF16), pltpu.VMEM((L, L), BF16), pltpu.VMEM((1, L), F32),
            pltpu.VMEM((R * S, L), BF16), pltpu.VMEM((R * S, L), BF16),
            pltpu.VMEM((R * S, L), BF16), pltpu.VMEM((R * S, L), BF16),
            pltpu.VMEM((2 * N, L), BF16), pltpu.VMEM((L, L), BF16),
            pltpu.VMEM((2 * N, ROWS), BF16), pltpu.VMEM((ROWS, 2 * N), BF16),
            pltpu.VMEM((CUTS, L), F32), pltpu.VMEM((ROWS, L), BF16), pltpu.VMEM((ROWS, L), F32),
            pltpu.VMEM((ROWS, L), F32), pltpu.VMEM((ROWS, L), BF16),
            pltpu.SemaphoreType.DMA((17,)),
            pltpu.SemaphoreType.DMA((R,)), pltpu.SemaphoreType.DMA((R,)),
            pltpu.SemaphoreType.DMA((R,)), pltpu.SemaphoreType.DMA((R,)),
        ],
        compiler_params=pltpu.CompilerParams(collective_id=0, has_side_effects=True),
        name="message_step",
    )(
        node_latent[0], edge_latent[0], cut_latent[0].reshape(CUTS, L), node_cotangent[0],
        edge_sender, edge_receiver, boundary_rows.reshape(R, 1, S), cut_slot.reshape(R, 1, C), cut_receiver.reshape(R, 1, C),
        node_count.reshape(1, 1), edge_count.reshape(1, 1),
        edge_first, edge_second, edge_gain.reshape(1, L), node_first, node_second,
        node_gain.reshape(1, L),
    )
    updated, gradient, edge_gradient, cut_gradient = pl.pallas_call(
        write_out,
        out_shape=tuple(jax.ShapeDtypeStruct((n, L), BF16) for n in (N, N, E, CUTS)),
        in_specs=[pl.BlockSpec(memory_space=pltpu.VMEM)] * 4,
        out_specs=(anyspec,) * 4,
        scratch_shapes=[pltpu.SemaphoreType.DMA((4,))],
        name="write_out",
    )(*(pltpu.with_memory_space_constraint(o, pltpu.VMEM) for o in outs))
    return updated[None], gradient[None], edge_gradient[None], cut_gradient.reshape(1, R, C, L)


def solution(mesh):
    part = ("grp", "dev")
    three = P(part, None, None)
    four = P(part, None, None, None)
    placed = (
        three, three, four, three, P(part, None), P(part, None), three, three, three, P(part),
        P(part), P(), P(), P(), P(), P(), P(),
    )
    return jax.shard_map(
        shards, mesh=mesh, in_specs=placed, out_specs=(three, three, three, four), check_vma=False,
    )
```

time: 27 us -> 26.4 us (0.978)
  Pallas kernels: 24.9 us -> 24.3 us
    pallas_call x1, Pallas kernels: 24.1 us -> 23.5 us  [shards(): pl.pallas_call(kernel, out_shape=tuple((pltpu.VMEM((n, L), BF16) for n in...]
where the time goes in v3:
time: 26.4 us; the launch traced here: 26.2 us
  Pallas kernels  24.3 us (92%)
  between operations  1.94 us (7%)
    pallas_call x1, Pallas kernels, shards(): pl.pallas_call(kernel, out_shape=tuple((pltpu.VMEM((n, L), BF16) for n in...  23.5 us
    pallas_call x1, Pallas kernels, shards(): pl.pallas_call(write_out, out_shape=tuple((jax.ShapeDtypeStruct((n, L), B...  0.81 us

profile of v3, /device:TPU:2, one launch (start us, length us, event | category | flops | bytes accessed | tf_op | source)
XLA Modules:
  0.0 26.2 jit_solution(12430922029443334982)
XLA Ops:
  1.9 23.5 %message_step.1 = (bf16[128,256]{1,0:T(8,128)(2,1)S(1)}, bf16[128,256]{1,0:T(8,128)(2,1)S(1)}, bf16[384,256]{1,0:T(8,128)(2,1)S(1)}, bf16[320,256]{1,0:T(8,128)(2,1)S(1)}) custom-call(bf16[128,256]{1,0:T(8,128)(2,1)} %bitcast.19, bf16[384,256]{1,0:T(8,128)(2,1)} %bitcast.17, bf16[320,256]{1,0:T(8,128)(2,1)} %bitcast.18, bf16[128,256]{1,0:T(8,128)(2,1)} %bitcast.20, ...), custom_call_target="tpu_custom_call" | custom-call | tf_op jit(solution)/shard_map/message_step/pallas_call | solution.py:255
  25.4 0.8 %write_out.1 = (bf16[128,256]{1,0:T(8,128)(2,1)}, bf16[128,256]{1,0:T(8,128)(2,1)}, bf16[384,256]{1,0:T(8,128)(2,1)}, bf16[320,256]{1,0:T(8,128)(2,1)}) custom-call(bf16[128,256]{1,0:T(8,128)(2,1)S(1)} %get-tuple-element.12.a, bf16[128,256]{1,0:T(8,128)(2,1)S(1)} %get-tuple-element.13.b, bf16[384,256]{1,0:T(8,128)(2,1)S(1)} %get-tuple-element.14.c, ...), custom_call_target="tpu_custom_call" | custom-call | tf_op jit(solution)/shard_map/write_out/pallas_call | solution.py:286

commit v4 on v3

--- a/solution.py
+++ b/solution.py
@@ -58,20 +58,6 @@
     return act, (1.0 + t) + act * (1.0 - t)
 
 
-def twice(a):
-    return jnp.concatenate([a, a], 1)
-
-
-def row_means(w):
-    mean = dot_nt(jnp.full((N, L), 1.0 / L, BF16), w)
-    high = mean.astype(BF16)
-    return jnp.concatenate([high, (mean - high.astype(F32)).astype(BF16)], 1)
-
-
-def centred(act, w, means):
-    return dot(act, w) - twice(dot_nt(twice(act), means))
-
-
 def total_of(a):
     return jnp.sum(a, axis=-1, keepdims=True)
 
@@ -80,7 +66,7 @@
     nodes_h, edges_h, cut_h, cot_h, send_h, recv_h, bound_h, slot_h, crecv_h, ncount_h, ecount_h,
     ef_h, es_h, eg_h, nf_h, ns_h, ng_h,
     upd, grad, egrad, cgrad,
-    nodes, edges, cut, cot, sendi, recvi, bound, slot, crecv, ncount, ecount,
+    nodes, edges, cut, cot, sendi, recvi, bound, slot, crecv,
     ef, es, eg, nf, ns, ng,
     out_rows, in_rows, out_sums, in_sums, comb, weh, oht, pick, part, xb, side, slope, gpe,
     in_sem, s1, r1, s2, r2,
@@ -108,7 +94,6 @@
         pl.semaphore_signal(barrier, inc=1, device_id=p, device_id_type=MESH)
     load("recv", recv_h, recvi)
     load("send", send_h, sendi)
-    load("ecount", ecount_h, ecount)
     load("ef", ef_h, ef)
     load("edges", edges_h, edges)
     load("es", es_h, es)
@@ -120,7 +105,6 @@
     load("ns", ns_h, ns)
     load("ng", ng_h, ng)
     load("cot", cot_h, cot)
-    load("ncount", ncount_h, ncount)
 
     eye = one_hot_t(lax.broadcasted_iota(jnp.int32, (1, N), 1))
 
@@ -151,16 +135,17 @@
         size = half.shape[0]
         rows = pl.ds(start, size)
         act, sl = silu_pair(half)
-        cent = centred(act.astype(BF16), es[...], edge_means)
+        cent = dot(act.astype(BF16), es[...])
+        cent = cent - total_of(cent) * (1.0 / L)
         inv = lax.rsqrt(total_of(cent * cent) * (1.0 / L) + EPS)
         xh = (cent * inv).astype(BF16)
         xb[rows, :] = xh
         slope[rows, :] = sl * inv
         return dot(oht[0:N, start:start + size], xh)
 
-    need("recv", "send", "ecount")
+    need("recv", "send")
     lane = lax.broadcasted_iota(jnp.int32, (1, E), 1)
-    oht[0:N, 0:E] = one_hot_t(jnp.where(lane < ecount[...], recvi[...], -1))
+    oht[0:N, 0:E] = one_hot_t(jnp.where(lane < ecount_h[0, 0], recvi[...], -1))
     oht[N:, 0:E] = one_hot_t(sendi[...])
     tables(0, E)
     need("ef")
@@ -169,21 +154,19 @@
     comb[0:N, :] = (dot(nodes[...], ef[0:L, :]) * 0.5).astype(BF16)
     comb[N:, :] = (dot(nodes[...], sender) * 0.5).astype(BF16)
     need("edges", "es")
-    edge_means = row_means(es[...])
     total = forward(0, dot(pick[0:E, :], comb[...]) + dot(edges[...], weh[...]))
 
-    need("crecv", "slot", "cut", "eg", "nf", "ns", "ng", "cot", "ncount")
+    need("crecv", "slot", "cut", "eg", "nf", "ns", "ng", "cot")
     oht[0:N, E:] = one_hot_t(jnp.concatenate([crecv[r] for r in range(R)], 1))
     oht[N:, E:] = one_hot_t(jnp.concatenate([slot[r] + S * r for r in range(R)], 1))
     tables(E, CUTS)
     part[...] = dot(pick[E:, 0:N], comb[0:N, :]) + dot(cut[...], weh[...])
     ohtb = one_hot_t(jnp.concatenate([bound[r] for r in range(R)], 1))
-    node_means = row_means(ns[...])
     pre_node_own = dot(nodes[...], nf[0:L, :])
     es_f = es[...].astype(F32)
     es_c = ((es_f - total_of(es_f) * (1.0 / L)) * (0.5 * eg[...])).astype(BF16)
     chain = dot(es_c, nf[L:, :]).astype(BF16)
-    live = lax.broadcasted_iota(jnp.int32, (N, 1), 0) < ncount[...]
+    live = lax.broadcasted_iota(jnp.int32, (N, 1), 0) < ncount_h[0, 0]
     gain = ng[...]
     mcot = jnp.where(live, cot[...].astype(F32), 0.0)
     dc = mcot * gain
@@ -196,8 +179,10 @@
     total = total + forward(E, part[...] + dot(pick[E:, N:], arrived))
 
     received = (total * eg[...]).astype(BF16)
+    side[E:, :] = dot_nt(xb[E:, :], es[...])
     act, sl = silu_pair(0.5 * (pre_node_own + dot(received, nf[L:, :])))
-    cent = centred(act.astype(BF16), ns[...], node_means)
+    cent = dot(act.astype(BF16), ns[...])
+    cent = cent - total_of(cent) * (1.0 / L)
     along = total_of(dc * cent) * (1.0 / L)
     ninv = lax.rsqrt(total_of(cent * cent) * (1.0 / L) + EPS)
     goo = (ninv * dc - cent * (ninv * ninv * ninv * along)).astype(BF16)
@@ -211,7 +196,6 @@
         m2 = total_of(dot_nt(xb[rows, :], gm) * to.astype(F32)) * (1.0 / L)
         gpe[rows, :] = ((dot(to, gm2) - m2 * side[rows, :]) * slope[rows, :]).astype(BF16)
 
-    side[E:, :] = dot_nt(xb[E:, :], es[...])
     backward(E, CUTS)
     out_sums[...] = dot(oht[N:N + R * S, E:], gpe[E:, :]).astype(BF16)
     second = exchange(out_sums, in_sums, s2, r2)
@@ -255,13 +239,12 @@
     outs = pl.pallas_call(
         kernel,
         out_shape=tuple(pltpu.VMEM((n, L), BF16) for n in (N, N, E, CUTS)),
-        in_specs=[anyspec] * 17,
+        in_specs=[anyspec] * 9 + [pl.BlockSpec(memory_space=pltpu.SMEM)] * 2 + [anyspec] * 6,
         out_specs=(pl.BlockSpec(memory_space=pltpu.VMEM),) * 4,
         scratch_shapes=[
             pltpu.VMEM((N, L), BF16), pltpu.VMEM((E, L), BF16), pltpu.VMEM((CUTS, L), BF16),
             pltpu.VMEM((N, L), BF16), pltpu.VMEM((1, E), i32), pltpu.VMEM((1, E), i32),
             pltpu.VMEM((R, 1, S), i32), pltpu.VMEM((R, 1, C), i32), pltpu.VMEM((R, 1, C), i32),
-            pltpu.VMEM((1, 1), i32), pltpu.VMEM((1, 1), i32),
             pltpu.VMEM((3 * L, L), BF16), pltpu.VMEM((L, L), BF16), pltpu.VMEM((1, L), F32),
             pltpu.VMEM((2 * L, L), BF16), pltpu.VMEM((L, L), BF16), pltpu.VMEM((1, L), F32),
             pltpu.VMEM((R * S, L), BF16), pltpu.VMEM((R * S, L), BF16),
@@ -270,7 +253,7 @@
             pltpu.VMEM((2 * N, ROWS), BF16), pltpu.VMEM((ROWS, 2 * N), BF16),
             pltpu.VMEM((CUTS, L), F32), pltpu.VMEM((ROWS, L), BF16), pltpu.VMEM((ROWS, L), F32),
             pltpu.VMEM((ROWS, L), F32), pltpu.VMEM((ROWS, L), BF16),
-            pltpu.SemaphoreType.DMA((17,)),
+            pltpu.SemaphoreType.DMA((15,)),
             pltpu.SemaphoreType.DMA((R,)), pltpu.SemaphoreType.DMA((R,)),
             pltpu.SemaphoreType.DMA((R,)), pltpu.SemaphoreType.DMA((R,)),
         ],

time: 26.4 us -> 26.4 us (level)
  no operation moved by 1% of the time
where the time goes in v4:
time: 26.4 us; the launch traced here: 26.2 us
  Pallas kernels  24.2 us (92%)
  between operations  1.94 us (7%)
    pallas_call x1, Pallas kernels, shards(): pl.pallas_call(kernel, out_shape=tuple((pltpu.VMEM((n, L), BF16) for n in...  23.4 us
    pallas_call x1, Pallas kernels, shards(): pl.pallas_call(write_out, out_shape=tuple((jax.ShapeDtypeStruct((n, L), B...  0.81 us

profile of v4, /device:TPU:2, one launch (start us, length us, event | category | flops | bytes accessed | tf_op | source)
XLA Modules:
  0.0 26.2 jit_solution(18089642806507455938)
XLA Ops:
  1.9 23.4 %message_step.1 = (bf16[128,256]{1,0:T(8,128)(2,1)S(1)}, bf16[128,256]{1,0:T(8,128)(2,1)S(1)}, bf16[384,256]{1,0:T(8,128)(2,1)S(1)}, bf16[320,256]{1,0:T(8,128)(2,1)S(1)}) custom-call(bf16[128,256]{1,0:T(8,128)(2,1)} %bitcast.19, bf16[384,256]{1,0:T(8,128)(2,1)} %bitcast.17, bf16[320,256]{1,0:T(8,128)(2,1)} %bitcast.18, bf16[128,256]{1,0:T(8,128)(2,1)} %bitcast.20, ...), custom_call_target="tpu_custom_call" | custom-call | tf_op jit(solution)/shard_map/message_step/pallas_call | solution.py:239
  25.4 0.8 %write_out.1 = (bf16[128,256]{1,0:T(8,128)(2,1)}, bf16[128,256]{1,0:T(8,128)(2,1)}, bf16[384,256]{1,0:T(8,128)(2,1)}, bf16[320,256]{1,0:T(8,128)(2,1)}) custom-call(bf16[128,256]{1,0:T(8,128)(2,1)S(1)} %get-tuple-element.12.a, bf16[128,256]{1,0:T(8,128)(2,1)S(1)} %get-tuple-element.13.b, bf16[384,256]{1,0:T(8,128)(2,1)S(1)} %get-tuple-element.14.c, ...), custom_call_target="tpu_custom_call" | custom-call | tf_op jit(solution)/shard_map/write_out/pallas_call | solution.py:269

commit v5 on v4

--- a/solution.py
+++ b/solution.py
@@ -106,8 +106,6 @@
     load("ng", ng_h, ng)
     load("cot", cot_h, cot)
 
-    eye = one_hot_t(lax.broadcasted_iota(jnp.int32, (1, N), 1))
-
     need("nodes", "bound")
     ohb = one_hot(column(lambda i: bound[i], R, S))
     out_rows[...] = dot(ohb, nodes[...]).astype(BF16)
@@ -129,7 +127,7 @@
     def tables(start, size):
         for b in range(start, start + size, N):
             n = min(N, start + size - b)
-            pick[b:b + n, :] = dot_nt(eye[:n, :n], oht[:, b:b + n]).astype(BF16)
+            pick[b:b + n, :] = oht[:, b:b + n].T
 
     def forward(start, half):
         size = half.shape[0]
@@ -209,11 +207,12 @@
     egrad[...] = dot_nt(gpe[0:E, :], latent_t).astype(BF16)
     rsum = dot(oht[0:N, :], gpe[...]).astype(BF16)
     base = base + dot_nt(rsum, ef[0:L, :])
-    ssum = dot(oht[N:, 0:E], gpe[0:E, :])
+    ssum = dot(oht[N:, 0:E], gpe[0:E, :]).astype(BF16)
+    base = base + dot_nt(ssum, sender)
     for c in second:
         c.wait_recv()
-    ssum = (ssum + dot(ohtb, in_sums[...])).astype(BF16)
-    grad[...] = (base + dot_nt(ssum, sender)).astype(BF16)
+    back = dot_nt(in_sums[...], sender).astype(BF16)
+    grad[...] = (base + dot(ohtb, back)).astype(BF16)
     for c in first + second:
         c.wait_send()
 

time: 26.4 us -> 26.4 us (level)
  no operation moved by 1% of the time
where the time goes in v5:
time: 26.4 us; the launch traced here: 26.2 us
  Pallas kernels  24.2 us (92%)
  between operations  1.94 us (7%)
    pallas_call x1, Pallas kernels, shards(): pl.pallas_call(kernel, out_shape=tuple((pltpu.VMEM((n, L), BF16) for n in...  23.4 us
    pallas_call x1, Pallas kernels, shards(): pl.pallas_call(write_out, out_shape=tuple((jax.ShapeDtypeStruct((n, L), B...  0.81 us

profile of v5, /device:TPU:2, one launch (start us, length us, event | category | flops | bytes accessed | tf_op | source)
XLA Modules:
  0.0 26.2 jit_solution(17725979050504202281)
XLA Ops:
  1.9 23.4 %message_step.1 = (bf16[128,256]{1,0:T(8,128)(2,1)S(1)}, bf16[128,256]{1,0:T(8,128)(2,1)S(1)}, bf16[384,256]{1,0:T(8,128)(2,1)S(1)}, bf16[320,256]{1,0:T(8,128)(2,1)S(1)}) custom-call(bf16[128,256]{1,0:T(8,128)(2,1)} %bitcast.19, bf16[384,256]{1,0:T(8,128)(2,1)} %bitcast.17, bf16[320,256]{1,0:T(8,128)(2,1)} %bitcast.18, bf16[128,256]{1,0:T(8,128)(2,1)} %bitcast.20, ...), custom_call_target="tpu_custom_call" | custom-call | tf_op jit(solution)/shard_map/message_step/pallas_call | solution.py:238
  25.4 0.8 %write_out.1 = (bf16[128,256]{1,0:T(8,128)(2,1)}, bf16[128,256]{1,0:T(8,128)(2,1)}, bf16[384,256]{1,0:T(8,128)(2,1)}, bf16[320,256]{1,0:T(8,128)(2,1)}) custom-call(bf16[128,256]{1,0:T(8,128)(2,1)S(1)} %get-tuple-element.12.a, bf16[128,256]{1,0:T(8,128)(2,1)S(1)} %get-tuple-element.13.b, bf16[384,256]{1,0:T(8,128)(2,1)S(1)} %get-tuple-element.14.c, ...), custom_call_target="tpu_custom_call" | custom-call | tf_op jit(solution)/shard_map/write_out/pallas_call | solution.py:268
